TPU v7x, 128 devices: a whole 4x4x4 slice. The times are simulated.
128 devices in a mesh: req: 4 (over x), hid: 32 (over y, z, core).
Axes of the slice: x: 4, y: 4, z: 4, core: 2. Of those that a mesh axis runs over, the one named last changes fastest.
Arguments:
- layer_input: bfloat16 [2048, 7168], P('req', 'hid'), may hold values from -6 to 6
- norm_gain: float32 [7168], replicated, may hold values from 0.1 to 1.9
- qkv_weight: bfloat16 [7168, 21504], P('req', 'hid'), may hold values from -0.09375 to 0.09375
- cache_keys: bfloat16 [4, 4096, 7168], P('req', None, 'hid'), may hold values from -160 to 160
- cache_values: bfloat16 [4, 4096, 7168], P('req', None, 'hid'), may hold values from -8 to 8
- cache_lengths: int32 [4], P('req'), may hold values from 1 to 4096, 10240 in all
- out_weight: bfloat16 [7168, 3584], P('hid'), may hold values from -0.375 to 0.375
- mlp_gain: float32 [3584], replicated, may hold values from 0.1 to 1.9
- gate_weight: bfloat16 [3584, 14336], P(None, 'hid'), may hold values from -0.09375 to 0.09375
- up_weight: bfloat16 [3584, 14336], P(None, 'hid'), may hold values from -0.09375 to 0.09375
- down_weight: bfloat16 [14336, 3584], P('hid'), may hold values from -0.046875 to 0.046875
Outputs:
- block_out: bfloat16 [2048, 3584], P(('req', 'hid'))
All inputs are finite; a program needn't handle non-finite values. No bound on the sum of `cache_lengths` on one device may be relied on, other than what follows from the above.
Results may differ from a plain program's by a relative error of at most 0.02.
Values may be sent and summed in bfloat16 or wider, within the bound.
A program may use at most 128 MiB of HBM per device.

v0:
```python
import jax
import jax.numpy as jnp
from jax import lax
from jax.sharding import PartitionSpec as P

D = 3584
HD = 224
epsilon = 1e-05


def rms_scale(values, gain):
    return values * lax.rsqrt(jnp.mean(values * values, axis=-1, keepdims=True) + epsilon) * gain


def rotate(values, position):
    half = values.shape[-1] // 2
    freq = jnp.exp(-jnp.log(10000.0) * 2.0 * jnp.arange(half, dtype=jnp.float32) / values.shape[-1])
    angle = position.astype(jnp.float32)[:, None, None] * freq[None, None, :]
    cosine = jnp.cos(angle)
    sine = jnp.sin(angle)
    first = values[..., :half]
    second = values[..., half:]
    return jnp.concatenate(
        [first * cosine - second * sine, second * cosine + first * sine], axis=-1
    )


def merge_block(carry, scores, values):
    top, total, accum = carry
    new_top = jnp.maximum(top, jnp.max(scores, axis=2))
    fade = jnp.exp(top - new_top)
    weights = jnp.exp(scores - new_top[:, :, None])
    total = total * fade + jnp.sum(weights, axis=2)
    accum = accum * fade.T[:, :, None] + jnp.einsum(
        "hqk,khd->qhd", weights.astype(jnp.bfloat16), values, preferred_element_type=jnp.float32
    )
    return (new_top, total, accum)


def shards(
    layer_input,
    norm_gain,
    qkv_weight,
    cache_keys,
    cache_values,
    cache_lengths,
    out_weight,
    mlp_gain,
    gate_weight,
    up_weight,
    down_weight,
):
    span = layer_input.shape[0]
    heads_dev = cache_keys.shape[2] // HD
    slots = cache_keys.shape[1]
    scale = HD ** (-0.5)
    whole_input = lax.all_gather(layer_input, "hid", axis=1, tiled=True)
    normed = rms_scale(whole_input.astype(jnp.float32), norm_gain).astype(jnp.bfloat16)
    columns = normed
    projected = jnp.dot(
        columns,
        lax.all_gather(qkv_weight, "req", axis=0, tiled=True),
        preferred_element_type=jnp.float32,
    ).reshape(span, heads_dev, 3, HD)
    length = cache_lengths[0]
    position = length + jnp.arange(span, dtype=jnp.int32)
    query = rotate(projected[:, :, 0], position).astype(jnp.bfloat16)
    fresh_keys = rotate(projected[:, :, 1], position).astype(jnp.bfloat16)
    fresh_values = projected[:, :, 2].astype(jnp.bfloat16)
    cache_k = cache_keys[0].reshape(slots, heads_dev, HD)
    cache_v = cache_values[0].reshape(slots, heads_dev, HD)
    block = min(512, slots)
    block_count = (length + block - 1) // block

    def visit(index, carry):
        keys = lax.dynamic_slice_in_dim(cache_k, index * block, block, 0)
        values = lax.dynamic_slice_in_dim(cache_v, index * block, block, 0)
        scores = jnp.einsum("qhd,khd->hqk", query, keys, preferred_element_type=jnp.float32) * scale
        columns = index * block + jnp.arange(block, dtype=jnp.int32)
        scores = jnp.where(columns[None, None, :] < length, scores, -1e30)
        return merge_block(carry, scores, values)

    start_state = (
        jnp.full((heads_dev, span), -1e30, jnp.float32),
        jnp.zeros((heads_dev, span), jnp.float32),
        jnp.zeros((span, heads_dev, HD), jnp.float32),
    )
    state = lax.fori_loop(0, block_count, visit, start_state)
    fresh_scores = (
        jnp.einsum("qhd,khd->hqk", query, fresh_keys, preferred_element_type=jnp.float32) * scale
    )
    causal = (
        jnp.arange(span, dtype=jnp.int32)[None, :] <= jnp.arange(span, dtype=jnp.int32)[:, None]
    )
    fresh_scores = jnp.where(causal[None, :, :], fresh_scores, -1e30)
    top, total, accum = merge_block(state, fresh_scores, fresh_values)
    heads_out = (accum / total.T[:, :, None]).astype(jnp.bfloat16).reshape(span, heads_dev * HD)
    row_count = span // lax.axis_size("hid")
    row_start = lax.axis_index("hid") * row_count
    attention = lax.psum(
        jnp.dot(heads_out, out_weight, preferred_element_type=jnp.float32).astype(jnp.bfloat16),
        "hid",
    ).astype(jnp.float32)
    mid = (whole_input[:, :D].astype(jnp.float32) + attention).astype(jnp.bfloat16)
    mlp_in = rms_scale(mid.astype(jnp.float32), mlp_gain).astype(jnp.bfloat16)
    gate = jnp.dot(mlp_in, gate_weight, preferred_element_type=jnp.float32)
    upward = jnp.dot(mlp_in, up_weight, preferred_element_type=jnp.float32)
    hidden = (jax.nn.gelu(gate, approximate=True) * upward).astype(jnp.bfloat16)
    mlp_part = lax.psum_scatter(
        jnp.dot(hidden, down_weight, preferred_element_type=jnp.float32).astype(jnp.bfloat16),
        "hid",
        scatter_dimension=0,
        tiled=True,
    ).astype(jnp.float32)
    mid_own = lax.dynamic_slice_in_dim(mid, row_start, row_count, 0)
    return (mid_own.astype(jnp.float32) + mlp_part).astype(jnp.bfloat16)


def solution(mesh):
    placed = (
        P("req", "hid"),
        P(),
        P("req", "hid"),
        P("req", None, "hid"),
        P("req", None, "hid"),
        P("req"),
        P("hid", None),
        P(),
        P(None, "hid"),
        P(None, "hid"),
        P("hid", None),
    )
    return jax.shard_map(
        shards, mesh=mesh, in_specs=placed, out_specs=P(("req", "hid"), None), check_vma=False
    )
```

profile of v0, /device:TPU:0, one launch (start us, length us, event | category | flops | bytes accessed | tf_op | source)
XLA Modules:
  0.0 435.5 jit_solution(8863642717574515305)
XLA Ops:
  6.5 0.7 all-gather.3.cloned.1.call-update
  7.3 0.7 all-gather.5.cloned.1.call-update
  8.8 54.3 %all-gather.3.cloned.1.call-done = bf16[512,7168]{0,1:T(8,128)(2,1)} async-done(((bf16[512,224]{0,1:T(8,128)(2,1)}), bf16[512,7168]{0,1:T(8,128)(2,1)}) %all-gather.3.cloned.1.call-update) | async-done | bytes 7340048 | tf_op jit(solution)/shard_map/all_gather | solution.py:57
  63.0 4.7 %fusion.13 = f32[512]{0:T(512)S(1)} fusion(bf16[512,7168]{0,1:T(8,128)(2,1)} %all-gather.3.cloned.1.call-done), kind=kLoop, calls=%fused_computation.20 | loop fusion | flops 11009536 | bytes 7342080 | tf_op jit(solution)/shard_map/reduce_sum | solution.py:12
  67.7 89.6 %all-gather.5.cloned.1.call-done = bf16[7168,672]{0,1:T(8,128)(2,1)} async-done(((bf16[1792,672]{0,1:T(8,128)(2,1)}), bf16[7168,672]{0,1:T(8,128)(2,1)}) %all-gather.5.cloned.1.call-update) | async-done | bytes 9633808 | tf_op jit(solution)/shard_map/all_gather | solution.py:62
  157.3 11.0 %fusion.19 = f32[512,672]{0,1:T(8,128)S(1)} fusion(bf16[7168,672]{0,1:T(8,128)(2,1)} %all-gather.5.cloned.1.call-done, bf16[512,7168]{0,1:T(8,128)(2,1)} %all-gather.3.cloned.1.call-done, f32[7168]{0:T(1024)S(1)} %copy-done.5, f32[512]{0:T(512)S(1)} %add_rsqrt_fusion.1), kind=kOutput, calls=%fused_computation.28 | convolution fusion | flops 4947181568 | bytes 18380800 | tf_op jit(solution)/shard_map/dot_general | solution.py:60
  168.4 1.7 fusion.78
  170.1 0.7 pad_maximum_fusion
  170.8 0.9 broadcast_in_dim.26
  171.7 13.9 %while.14 = (s32[]{:T(128)}, f32[1,512]{1,0:T(1,128)S(1)}, f32[1,512]{1,0:T(1,128)S(1)}, f32[512,1,224]{0,2,1:T(8,128)}, s32[]{:T(128)}, /*index=5*/s32[]{:T(128...) while((s32[]{:T(128)}, f32[1,512]{1,0:T(1,128)S(1)}, ...), condition=%wide.region_4.5_spmd, body=%wide.region_1.4_spmd.sunk | while | flops 236947456 | bytes 4785347 | solution.py:88
  171.7 0.7 add_compare_fusion.2
  172.4 1.4 fusion.94
  174.0 2.3 fusion.96
  176.3 0.7 add_compare_fusion.2
  177.0 1.4 fusion.94
  178.6 2.3 fusion.96
  181.0 0.7 add_compare_fusion.2
  181.6 1.4 fusion.94
  183.3 2.3 fusion.96
  185.6 1.3 fusion.81
  187.0 1.0 copy-done.1
  188.2 5.3 %convolution_convert_fusion = bf16[512,3584]{1,0:T(8,128)(2,1)} fusion(bf16[224,3584]{1,0:T(8,128)(2,1)} %param.19, f32[512,512]{0,1:T(8,128)} %copy-done.1, f32[512]{0:T(512)S(1)} %bitcast.98, f32[512,1,224]{0,2,1:T(8,128)} %get-tuple-element.55, f32[512,1,3,224]{0,3,2,1:T(8,128)} %bitcast.88, f32[512]{0:T(512)S(1)} %bitcast.100, f32[512]{0:T(512)S(1)} %bitcast.101), kind=kOutput, calls=%fused_computation.32 | convolution fusion | flops 942342144 | bytes 7018496 | tf_op jit(solution)/shard_map/dot_general | solution.py:101
  193.5 0.2 reduce-scatter.2.cloned.1.call-start
  193.7 4.1 slice.33
  197.8 5.9 %copy.21 = bf16[512,3584]{1,0:T(8,128)(2,1)} copy(bf16[512,3584]{0,1:T(8,128)(2,1)} %slice.33) | data formatting | bytes 7340032
  203.8 123.4 %all-reduce.2.cloned.1.call-done = bf16[512,3584]{1,0:T(8,128)(2,1)} async-done(((bf16[512,3584]{1,0:T(8,128)(2,1)}), bf16[512,3584]{1,0:T(8,128)(2,1)}) %all-reduce.2.cloned.1.call-update) | async-done | bytes 3670032 | tf_op jit(solution)/shard_map/psum | solution.py:100
  327.2 4.9 %fusion.16 = (f32[512]{0:T(512)S(1)}, bf16[512,3584]{1,0:T(8,128)(2,1)S(1)}) fusion(bf16[512,3584]{1,0:T(8,128)(2,1)} %all-reduce.2.cloned.1.call-done, bf16[512,3584]{1,0:T(8,128)(2,1)} %copy.21), kind=kLoop, calls=%fused_computation.25 | loop fusion | flops 12844544 | bytes 11012096 | tf_op jit(solution)/shard_map/reduce_sum | solution.py:12
  332.1 1.8 copy-done.2
  333.9 3.1 fusion.40
  337.0 9.0 %convolution_convert_fusion.1 = bf16[512,3584]{1,0:T(8,128)(2,1)} fusion(bf16[448,3584]{1,0:T(8,128)(2,1)S(1)} %copy-done, f32[512,448]{0,1:T(8,128)} %fusion.40, bf16[3584,448]{0,1:T(8,128)(2,1)} %param.22, bf16[512,3584]{1,0:T(8,128)(2,1)} %copy-done.2, f32[3584]{0:T(1024)S(1)} %copy-done.6, f32[512]{0:T(512)S(1)} %add_rsqrt_fusion), kind=kOutput, calls=%fused_computation.33 | convolution fusion | flops 3297968128 | bytes 14696448 | tf_op jit(solution)/shard_map/dot_general | solution.py:110
  346.0 81.3 %reduce-scatter.2.cloned.1.call-done = bf16[16,3584]{1,0:T(8,128)(2,1)} async-done(((bf16[512,3584]{1,0:T(8,128)(2,1)}), bf16[16,3584]{1,0:T(8,128)(2,1)}) %reduce-scatter.2.cloned.1.call-update) | async-done | bytes 114704 | tf_op jit(solution)/shard_map/reduce_scatter | solution.py:109
  427.4 1.6 add_convert_fusion.1
  (39 shorter events, 1.1 us)
Async XLA Ops:
  6.5 330.5 %copy-start = (bf16[448,3584]{1,0:T(8,128)(2,1)S(1)}, bf16[448,3584]{1,0:T(8,128)(2,1)}, u32[]{:S(2)}) copy-start(bf16[448,3584]{1,0:T(8,128)(2,1)} %param.23) | copy-start | bytes 9633796
  6.5 56.5 %all-gather.3.cloned.1.call-start = ((), (), s32[]{:S(2)}) async-start(), calls=%async_computation.1 | async-start | bytes 7569408 | tf_op jit(solution)/shard_map/all_gather | solution.py:57
  7.3 150.0 %all-gather.5.cloned.1.call-start = ((), (), s32[]{:S(2)}) async-start(), calls=%async_computation.2 | async-start | bytes 12042240 | tf_op jit(solution)/shard_map/all_gather | solution.py:62
  8.0 319.2 %all-reduce.2.cloned.1.call-start = ((), (), s32[]{:S(2)}) async-start(), calls=%async_computation.3 | async-start | bytes 7340032 | tf_op jit(solution)/shard_map/psum | solution.py:100
  8.7 148.6 %copy-start.5 = (f32[7168]{0:T(1024)S(1)}, f32[7168]{0:T(1024)}, u32[]{:S(2)}) copy-start(f32[7168]{0:T(1024)} %param.14) | copy-start | bytes 86020
  168.3 1.8 copy-start.3
  186.9 1.0 copy-start.1
  193.5 233.9 %reduce-scatter.2.cloned.1.call-start = ((), (), s32[]{:S(2)}) async-start(), calls=%async_computation.4 | async-start | bytes 3784704 | tf_op jit(solution)/shard_map/reduce_scatter | solution.py:109
  203.7 130.1 %copy-start.6 = (f32[3584]{0:T(1024)S(1)}, f32[3584]{0:T(1024)}, u32[]{:S(2)}) copy-start(f32[3584]{0:T(1024)} %param.20) | copy-start | bytes 43012
  327.2 6.7 %copy-start.4 = (bf16[3584,448]{0,1:T(8,128)(2,1)S(1)}, bf16[3584,448]{0,1:T(8,128)(2,1)}, u32[]{:S(2)}) copy-start(bf16[3584,448]{0,1:T(8,128)(2,1)} %param.21) | copy-start | bytes 9633796
  332.1 1.8 copy-start.2
Sparse Core Ops, SparseCore 0:
  9.6 53.3 all-gather.2
  64.7 92.5 all-gather.4
  193.6 133.5 all-reduce.1
  346.1 81.1 reduce-scatter.1
where the time goes:
time: 436 us
  waiting for transfers between devices  350 us (80%)
  matrix products  41 us (9%)
  other arithmetic  16.4 us (4%)
  between operations  13.9 us (3%)
  local copies, waits for them, and re-layouts  13.8 us (3%)
    psum x1, waiting for transfers between devices, shards(): lax.psum(jnp.dot(heads_out, out_weight, preferred_element_type=jnp.float3...  123 us
    all_gather x1, waiting for transfers between devices, shards(): lax.all_gather(qkv_weight, 'req', axis=0, tiled=True)  89.6 us
    reduce_scatter x1, waiting for transfers between devices, shards(): lax.psum_scatter(jnp.dot(hidden, down_weight, preferred_element_type=jnp....  81.3 us
    all_gather x1, waiting for transfers between devices, shards(): whole_input = lax.all_gather(layer_input, 'hid', axis=1, tiled=True)  54.3 us
    dot_general x1, matrix products, shards(): jnp.dot(columns, lax.all_gather(qkv_weight, 'req', axis=0, tiled=True), p...  11 us
    reduce_sum x2, other arithmetic, rms_scale(): jnp.mean(values * values, axis=-1, keepdims=True) + epsilon  9.55 us
    dot_general x1, matrix products, shards(): jnp.dot(hidden, down_weight, preferred_element_type=jnp.float32)  8.99 us
    unnamed x15, local copies, waits for them, and re-layouts  8.73 us
  transfers between devices with their start and end apart: 4, of which 4 were waited for; matrix products, arithmetic and copies ran while one was open for 3% of the time, Pallas kernels for 0%

commit v1 on v0

--- a/solution.py
+++ b/solution.py
@@ -6,6 +6,13 @@
 D = 3584
 HD = 224
 epsilon = 1e-05
+
+
+def exchange_gather(x, axis, along):
+    size = lax.axis_size(axis)
+    pieces = jnp.stack([x for _ in range(size)])
+    pieces = lax.all_to_all(pieces, axis, split_axis=0, concat_axis=0)
+    return jnp.concatenate(pieces, axis=along)
 
 
 def rms_scale(values, gain):
@@ -54,7 +61,7 @@
     heads_dev = cache_keys.shape[2] // HD
     slots = cache_keys.shape[1]
     scale = HD ** (-0.5)
-    whole_input = lax.all_gather(layer_input, "hid", axis=1, tiled=True)
+    whole_input = exchange_gather(layer_input, "hid", 1)
     normed = rms_scale(whole_input.astype(jnp.float32), norm_gain).astype(jnp.bfloat16)
     columns = normed
     projected = jnp.dot(

time: 436 us -> 418 us (0.959)
  waiting for transfers between devices: 350 us -> 312 us
  starting transfers between devices: 0.3 us -> 8.96 us
  other arithmetic: 16.4 us -> 24 us
  local copies, waits for them, and re-layouts: 13.8 us -> 18.8 us
    all_to_all x0 -> x1, waiting for transfers between devices: none -> 97.5 us  [exchange_gather(): pieces = lax.all_to_all(pieces, axis, split_axis=0, concat_axis=0)]
    all_gather x1, waiting for transfers between devices: 89.6 us -> 0.01 us  [shards(): lax.all_gather(qkv_weight, 'req', axis=0, tiled=True)]
    all_gather x1 -> x0, waiting for transfers between devices: 54.3 us -> none  [shards(): whole_input = lax.all_gather(layer_input, 'hid', axis=1, tiled=True)]
    psum x1, waiting for transfers between devices: 123 us -> 132 us  [shards(): lax.psum(jnp.dot(heads_out, out_weight, preferred_element_type=jnp.float3...]
    all_to_all x0 -> x1, starting transfers between devices: none -> 8.69 us  [exchange_gather(): pieces = lax.all_to_all(pieces, axis, split_axis=0, concat_axis=0)]
    convert_element_type x0 -> x1, other arithmetic: none -> 7.15 us  [shards(): rms_scale(whole_input.astype(jnp.float32), norm_gain).astype(jnp.bfloat16)]
    another operation x0 -> x1, local copies, waits for them, and re-layouts: none -> 4.95 us  [exchange_gather(): pieces = jnp.stack([x for _ in range(size)])]
  transfers between devices with their start and end apart: 4 -> 4, of which waited for: 4 -> 3; matrix products, arithmetic and copies ran while one was open for 3% -> 7% of each run, Pallas kernels for 0% -> 0%
where the time goes in v1:
time: 418 us; the launch traced here: 417 us
  waiting for transfers between devices  312 us (75%)
  matrix products  39.7 us (9%)
  other arithmetic  24 us (6%)
  local copies, waits for them, and re-layouts  18.8 us (4%)
  between operations  13.9 us (3%)
  starting transfers between devices  8.96 us (2%)
    psum x1, waiting for transfers between devices, shards(): lax.psum(jnp.dot(heads_out, out_weight, preferred_element_type=jnp.float3...  132 us
    all_to_all x1, waiting for transfers between devices, exchange_gather(): pieces = lax.all_to_all(pieces, axis, split_axis=0, concat_axis=0)  97.5 us
    reduce_scatter x1, waiting for transfers between devices, shards(): lax.psum_scatter(jnp.dot(hidden, down_weight, preferred_element_type=jnp....  81.4 us
    reduce_sum x2, other arithmetic, rms_scale(): jnp.mean(values * values, axis=-1, keepdims=True) + epsilon  9.93 us
    dot_general x1, matrix products, shards(): jnp.dot(columns, lax.all_gather(qkv_weight, 'req', axis=0, tiled=True), p...  9.86 us
    dot_general x1, matrix products, shards(): jnp.dot(hidden, down_weight, preferred_element_type=jnp.float32)  8.99 us
    unnamed x15, local copies, waits for them, and re-layouts  8.76 us
    all_to_all x1, starting transfers between devices, exchange_gather(): pieces = lax.all_to_all(pieces, axis, split_axis=0, concat_axis=0)  8.69 us
  transfers between devices with their start and end apart: 4, of which 3 were waited for; matrix products, arithmetic and copies ran while one was open for 7% of the time, Pallas kernels for 0%

profile of v1, /device:TPU:0, one launch (start us, length us, event | category | flops | bytes accessed | tf_op | source)
XLA Modules:
  0.0 417.1 jit_solution(17828438280275467870)
XLA Ops:
  6.5 0.7 all-gather.2.cloned.1.call-update
  7.3 4.9 %stack.2 = bf16[32,512,224]{1,2,0:T(8,128)(2,1)} broadcast(bf16[512,224]{0,1:T(8,128)(2,1)} %param.13), dimensions={1,2} | broadcast | bytes 7569408 | tf_op jit(solution)/shard_map/stack | solution.py:13
  12.2 8.7 %all-to-all-start = ((bf16[32,512,224]{1,2,0:T(8,128)(2,1)}), bf16[32,512,224]{1,2,0:T(8,128)(2,1)}, u32[]{:S(2)}, u32[]{:S(2)}) async-start(bf16[32,512,224]{1,2,0:T(8,128)(2,1)} %stack.2), calls=%async_computation | async-start | bytes 14680064 | tf_op jit(solution)/shard_map/all_to_all | solution.py:14
  21.7 97.5 %all-to-all-done = bf16[32,512,224]{1,2,0:T(8,128)(2,1)} async-done(((bf16[32,512,224]{1,2,0:T(8,128)(2,1)}), bf16[32,512,224]{1,2,0:T(8,128)(2,1)}, u32[]{:S(2)}, u32[]{:S(2)}) %all-to-all-start) | async-done | bytes 7340064 | tf_op jit(solution)/shard_map/all_to_all | solution.py:14
  119.2 5.0 %fusion.13 = f32[512]{0:T(512)S(1)} fusion(bf16[32,512,224]{1,2,0:T(8,128)(2,1)} %all-to-all-done), kind=kLoop, calls=%fused_computation.20 | loop fusion | flops 11009536 | bytes 7342080 | tf_op jit(solution)/shard_map/reduce_sum | solution.py:19
  124.2 7.1 %fusion.15 = bf16[512,32,224]{0,2,1:T(8,128)(2,1)} fusion(bf16[32,512,224]{1,2,0:T(8,128)(2,1)} %all-to-all-done, f32[32,224]{1,0:T(8,128)S(1)} %mul.172, f32[512]{0:T(512)S(1)} %add_rsqrt_fusion.1), kind=kLoop, calls=%fused_computation.22 | loop fusion | flops 14680064 | bytes 14710784 | tf_op jit(solution)/shard_map/convert_element_type | solution.py:65
  131.4 9.9 %convolution_bitcast_fusion.1 = f32[512,1,3,224]{0,3,2,1:T(8,128)S(1)} fusion(bf16[512,7168,1]{0,1,2:T(8,128)(2,1)} %bitcast.100, bf16[3,224,7168]{2,1,0:T(8,128)(2,1)} %bitcast.115), kind=kOutput, calls=%fused_computation.31 | convolution fusion | flops 4932501504 | bytes 18350080 | tf_op jit(solution)/shard_map/dot_general | solution.py:67
  141.3 1.7 fusion.74
  143.0 0.7 pad_maximum_fusion
  143.8 0.8 broadcast_in_dim.26
  144.6 13.8 %while.14 = (s32[]{:T(128)}, f32[1,512]{1,0:T(1,128)S(1)}, f32[1,512]{1,0:T(1,128)S(1)}, f32[512,1,224]{0,2,1:T(8,128)}, s32[]{:T(128)}, /*index=5*/s32[]{:T(128...) while((s32[]{:T(128)}, f32[1,512]{1,0:T(1,128)S(1)}, ...), condition=%wide.region_4.5_spmd, body=%wide.region_1.4_spmd.sunk | while | flops 236947456 | bytes 4785347 | solution.py:95
  144.6 0.7 add_compare_fusion.2
  145.3 1.4 fusion.91
  146.9 2.3 fusion.93
  149.2 0.7 add_compare_fusion.2
  149.9 1.4 fusion.91
  151.5 2.3 fusion.93
  153.8 0.7 add_compare_fusion.2
  154.5 1.4 fusion.91
  156.1 2.3 fusion.93
  158.4 1.3 fusion.77
  159.7 1.0 copy-done.1
  160.9 5.3 %convolution_convert_fusion = bf16[512,3584]{1,0:T(8,128)(2,1)} fusion(bf16[224,3584]{1,0:T(8,128)(2,1)} %param.19, f32[512,512]{0,1:T(8,128)} %copy-done.1, f32[512]{0:T(512)S(1)} %bitcast.110, f32[512,1,224]{0,2,1:T(8,128)} %get-tuple-element.55, f32[512,1,3,224]{0,3,2,1:T(8,128)} %copy-done.3, f32[512]{0:T(512)S(1)} %bitcast.112, f32[512]{0:T(512)S(1)} %bitcast.113), kind=kOutput, calls=%fused_computation.29 | convolution fusion | flops 942342144 | bytes 7018496 | tf_op jit(solution)/shard_map/dot_general | solution.py:108
  166.5 4.1 slice.33
  170.5 6.0 %copy.20 = bf16[512,3584]{1,0:T(8,128)(2,1)} copy(bf16[512,3584]{0,1:T(8,128)(2,1)} %slice.33) | data formatting | bytes 7340032
  176.5 132.2 %all-reduce.2.cloned.1.call-done = bf16[512,3584]{1,0:T(8,128)(2,1)} async-done(((bf16[512,3584]{1,0:T(8,128)(2,1)}), bf16[512,3584]{1,0:T(8,128)(2,1)}) %all-reduce.2.cloned.1.call-update) | async-done | bytes 3670032 | tf_op jit(solution)/shard_map/psum | solution.py:107
  308.8 4.9 %fusion.16 = (f32[512]{0:T(512)S(1)}, bf16[512,3584]{1,0:T(8,128)(2,1)S(1)}) fusion(bf16[512,3584]{1,0:T(8,128)(2,1)} %all-reduce.2.cloned.1.call-done, bf16[512,3584]{1,0:T(8,128)(2,1)} %copy.20), kind=kLoop, calls=%fused_computation.25 | loop fusion | flops 12844544 | bytes 11012096 | tf_op jit(solution)/shard_map/reduce_sum | solution.py:19
  313.7 1.8 copy-done.2
  315.5 3.1 fusion.36
  318.6 9.0 %convolution_convert_fusion.1 = bf16[512,3584]{1,0:T(8,128)(2,1)} fusion(bf16[448,3584]{1,0:T(8,128)(2,1)S(1)} %copy-done, f32[512,448]{0,1:T(8,128)} %fusion.36, bf16[3584,448]{0,1:T(8,128)(2,1)} %param.22, bf16[512,3584]{1,0:T(8,128)(2,1)} %copy-done.2, f32[3584]{0:T(1024)S(1)} %copy-done.6, f32[512]{0:T(512)S(1)} %add_rsqrt_fusion), kind=kOutput, calls=%fused_computation.30 | convolution fusion | flops 3297968128 | bytes 14696448 | tf_op jit(solution)/shard_map/dot_general | solution.py:117
  327.6 81.4 %reduce-scatter.2.cloned.1.call-done = bf16[16,3584]{1,0:T(8,128)(2,1)} async-done(((bf16[512,3584]{1,0:T(8,128)(2,1)}), bf16[16,3584]{1,0:T(8,128)(2,1)}) %reduce-scatter.2.cloned.1.call-update) | async-done | bytes 114704 | tf_op jit(solution)/shard_map/reduce_scatter | solution.py:116
  409.0 1.6 add_convert_fusion.1
  (41 shorter events, 1.4 us)
Async XLA Ops:
  6.5 312.1 %copy-start = (bf16[448,3584]{1,0:T(8,128)(2,1)S(1)}, bf16[448,3584]{1,0:T(8,128)(2,1)}, u32[]{:S(2)}) copy-start(bf16[448,3584]{1,0:T(8,128)(2,1)} %param.23) | copy-start | bytes 9633796
  6.5 124.9 %all-gather.2.cloned.1.call-start = ((), (), s32[]{:S(2)}) async-start(), calls=%async_computation.2 | async-start | bytes 12042240 | tf_op jit(solution)/shard_map/all_gather | solution.py:69
  12.2 9.4 %copy-start.4 = (f32[7168]{0:T(1024)S(1)}, f32[7168]{0:T(1024)}, u32[]{:S(2)}) copy-start(f32[7168]{0:T(1024)} %param.14) | copy-start | bytes 86020
  12.2 107.0 %all-to-all-start = ((bf16[32,512,224]{1,2,0:T(8,128)(2,1)}), bf16[32,512,224]{1,2,0:T(8,128)(2,1)}, u32[]{:S(2)}, u32[]{:S(2)}) async-start(bf16[32,512,224]{1,2,0:T(8,128)(2,1)} %stack.2), calls=%async_computation | async-start | bytes 14680064 | tf_op jit(solution)/shard_map/all_to_all | solution.py:14
  20.9 287.9 %all-reduce.2.cloned.1.call-start = ((), (), s32[]{:S(2)}) async-start(), calls=%async_computation.3 | async-start | bytes 7340032 | tf_op jit(solution)/shard_map/psum | solution.py:107
  141.3 1.8 copy-start.3
  159.7 1.0 copy-start.1
  166.2 242.7 %reduce-scatter.2.cloned.1.call-start = ((), (), s32[]{:S(2)}) async-start(), calls=%async_computation.4 | async-start | bytes 3784704 | tf_op jit(solution)/shard_map/reduce_scatter | solution.py:116
  176.5 138.9 %copy-start.6 = (f32[3584]{0:T(1024)S(1)}, f32[3584]{0:T(1024)}, u32[]{:S(2)}) copy-start(f32[3584]{0:T(1024)} %param.20) | copy-start | bytes 43012
  308.8 6.7 %copy-start.5 = (bf16[3584,448]{0,1:T(8,128)(2,1)S(1)}, bf16[3584,448]{0,1:T(8,128)(2,1)}, u32[]{:S(2)}) copy-start(bf16[3584,448]{0,1:T(8,128)(2,1)} %param.21) | copy-start | bytes 9633796
  313.7 1.8 copy-start.2
Sparse Core Ops, SparseCore 0:
  9.0 96.0 all-gather.1
  166.3 142.3 all-reduce.1
  327.7 81.1 reduce-scatter.1
